TPU v7x, 256 devices: a whole 4x4x8 slice. The times are simulated.
256 devices in a mesh: pl: 16 (over y, x), xs: 16 (over z, core).
Axes of the slice: x: 4, y: 4, z: 8, core: 2. Of those that a mesh axis runs over, the one named last changes fastest.
Arguments:
- source: float32 [512, 16, 2048], P('xs', None, 'pl'), may hold values from -6 to 6
- eastward_rate: float32 [512, 16, 2048], P('xs', None, 'pl'), may hold values from 300 to 6000
- northward_rate: float32 [512, 16, 2048], P('xs', None, 'pl'), may hold values from 300 to 6000
- vertical_rate: float32 [512, 16, 2048], P('xs', None, 'pl'), may hold values from 0.5 to 20
- amplitude: float32 [512, 16, 2048], P('xs', None, 'pl'), may hold values from 300 to 3000
Outputs:
- smoothed: float32 [512, 16, 2048], P('xs', None, 'pl')
All inputs are finite; a program needn't handle non-finite values.
Results may differ from a plain program's by a relative error of at most 0.0003.
Values sent between devices are 32-bit elements; how exact they have to be, the bound alone decides.
A program may use at most 128 MiB of HBM per device.

v0:
```python
import jax
import jax.numpy as jnp
from jax import lax
from jax.sharding import PartitionSpec as P


def cyclic(sub_band, centre, super_band, values):
    length = centre.shape[0]
    if length == 1:
        return values / centre

    def halves(operand):
        paired = operand.reshape((length // 2, 2) + operand.shape[1:])
        return (paired[:, 0], paired[:, 1])

    def following(operand, filler):
        return jnp.concatenate([operand[1:], jnp.full_like(operand[:1], filler)], axis=0)

    sub_even, sub_odd = halves(sub_band)
    centre_even, centre_odd = halves(centre)
    super_even, super_odd = halves(super_band)
    values_even, values_odd = halves(values)
    left_factor = -sub_odd / centre_even
    right_factor = -super_odd / following(centre_even, 1.0)
    reduced = cyclic(
        left_factor * sub_even,
        centre_odd + left_factor * super_even + right_factor * following(sub_even, 0.0),
        right_factor * following(super_even, 0.0),
        values_odd + left_factor * values_even + right_factor * following(values_even, 0.0),
    )
    previous = jnp.concatenate([jnp.zeros_like(reduced[:1]), reduced[:-1]], axis=0)
    even_part = (values_even - sub_even * previous - super_even * reduced) / centre_even
    return jnp.stack([even_part, reduced], axis=1).reshape((length,) + even_part.shape[1:])


def cyclic_last(sub_band, centre, super_band, values):
    length = centre.shape[-1]
    if length == 1:
        return values / centre

    def halves(operand):
        paired = operand.reshape(operand.shape[:-1] + (length // 2, 2))
        return (paired[..., 0], paired[..., 1])

    def following(operand, filler):
        return jnp.concatenate([operand[..., 1:], jnp.full_like(operand[..., :1], filler)], axis=-1)

    sub_even, sub_odd = halves(sub_band)
    centre_even, centre_odd = halves(centre)
    super_even, super_odd = halves(super_band)
    values_even, values_odd = halves(values)
    left_factor = -sub_odd / centre_even
    right_factor = -super_odd / following(centre_even, 1.0)
    reduced = cyclic_last(
        left_factor * sub_even,
        centre_odd + left_factor * super_even + right_factor * following(sub_even, 0.0),
        right_factor * following(super_even, 0.0),
        values_odd + left_factor * values_even + right_factor * following(values_even, 0.0),
    )
    previous = jnp.concatenate([jnp.zeros_like(reduced[..., :1]), reduced[..., :-1]], axis=-1)
    even_part = (values_even - sub_even * previous - super_even * reduced) / centre_even
    return jnp.stack([even_part, reduced], axis=-1).reshape(even_part.shape[:-1] + (length,))


def band_solve(values, rate_lines):
    length = values.shape[0]
    position = lax.broadcasted_iota(jnp.int32, rate_lines.shape, 0)
    sub_band = jnp.where(position > 0, -rate_lines, 0.0)
    super_band = jnp.where(position < length - 1, -rate_lines, 0.0)
    return cyclic(sub_band, 1.0 + 2.0 * rate_lines, super_band, values)


def vertical_solve(values, vertical_lines):
    return jnp.moveaxis(band_solve(jnp.moveaxis(values, 1, 0), vertical_lines), 0, 1)


def northward_solve(values, north_lines):
    length = values.shape[-1]
    position = lax.broadcasted_iota(jnp.int32, north_lines.shape, 2)
    sub_band = jnp.where(position > 0, -north_lines, 0.0)
    super_band = jnp.where(position < length - 1, -north_lines, 0.0)
    return cyclic_last(sub_band, 1.0 + 2.0 * north_lines, super_band, values)


def to_lines(values):
    return lax.all_to_all(values, "pl", split_axis=1, concat_axis=2, tiled=True)


def to_planes(values):
    return lax.all_to_all(values, "pl", split_axis=2, concat_axis=1, tiled=True)


def matrix_product(left_matrix, right_matrix):
    return (
        left_matrix[0] * right_matrix[0] + left_matrix[1] * right_matrix[2],
        left_matrix[0] * right_matrix[1] + left_matrix[1] * right_matrix[3],
        left_matrix[2] * right_matrix[0] + left_matrix[3] * right_matrix[2],
        left_matrix[2] * right_matrix[1] + left_matrix[3] * right_matrix[3],
    )


def matrix_inverse(matrix):
    determinant = matrix[0] * matrix[3] - matrix[1] * matrix[2]
    return (
        matrix[3] / determinant,
        -matrix[1] / determinant,
        -matrix[2] / determinant,
        matrix[0] / determinant,
    )


def matrix_vector(matrix, vector):
    return (
        matrix[0] * vector[0] + matrix[1] * vector[1],
        matrix[2] * vector[0] + matrix[3] * vector[1],
    )


def unpack_rows(packed):
    sub_block = (packed[0], packed[1], packed[2], packed[3])
    centre = (packed[4] + 1.0, packed[5], packed[6], packed[7] + 1.0)
    super_block = (packed[8], packed[9], packed[10], packed[11])
    right_side = (packed[12], packed[13])
    return (sub_block, centre, super_block, right_side)


def pack_rows(sub_block, centre, super_block, right_side):
    return jnp.stack(
        [
            sub_block[0],
            sub_block[1],
            sub_block[2],
            sub_block[3],
            centre[0] - 1.0,
            centre[1],
            centre[2],
            centre[3] - 1.0,
            super_block[0],
            super_block[1],
            super_block[2],
            super_block[3],
            right_side[0],
            right_side[1],
        ]
    )


def first_rows(boundary):
    blank_rows = jnp.zeros_like(boundary[0])
    return jnp.stack(
        [
            blank_rows,
            boundary[0],
            blank_rows,
            boundary[1],
            blank_rows,
            blank_rows,
            blank_rows,
            blank_rows,
            boundary[2],
            blank_rows,
            boundary[3],
            blank_rows,
            boundary[4],
            boundary[5],
        ]
    )


def eliminate(own_rows, rows_below, rows_above):
    sub_block, centre, super_block, right_side = unpack_rows(own_rows)
    sub_below, centre_below, super_below, right_below = unpack_rows(rows_below)
    sub_above, centre_above, super_above, right_above = unpack_rows(rows_above)
    left_factor = matrix_product(sub_block, matrix_inverse(centre_below))
    right_factor = matrix_product(super_block, matrix_inverse(centre_above))
    new_sub = tuple((-entry for entry in matrix_product(left_factor, sub_below)))
    new_super = tuple((-entry for entry in matrix_product(right_factor, super_above)))
    left_part = matrix_product(left_factor, super_below)
    right_part = matrix_product(right_factor, sub_above)
    new_centre = tuple((centre[slot] - left_part[slot] - right_part[slot] for slot in range(4)))
    left_vector = matrix_vector(left_factor, right_below)
    right_vector = matrix_vector(right_factor, right_above)
    new_right = (
        right_side[0] - left_vector[0] - right_vector[0],
        right_side[1] - left_vector[1] - right_vector[1],
    )
    return pack_rows(new_sub, new_centre, new_super, new_right)


def finish_rows(packed):
    sub_block, centre, super_block, right_side = unpack_rows(packed)
    return matrix_vector(matrix_inverse(centre), right_side)


def solve_gathered(gathered, own_index, devices):
    row_blocks = first_rows(jnp.moveaxis(gathered, 0, 1))
    stride = 1
    while stride < devices:
        blank_rows = jnp.zeros_like(row_blocks[:, :stride])
        rows_below = jnp.concatenate([blank_rows, row_blocks[:, :-stride]], axis=1)
        rows_above = jnp.concatenate([row_blocks[:, stride:], blank_rows], axis=1)
        row_blocks = eliminate(row_blocks, rows_below, rows_above)
        stride = stride * 2
    first_value, last_value = finish_rows(row_blocks)
    blank_value = jnp.zeros_like(first_value[:1])
    padded_first = jnp.concatenate([blank_value, first_value, blank_value], axis=0)
    padded_last = jnp.concatenate([blank_value, last_value, blank_value], axis=0)
    last_before = lax.dynamic_index_in_dim(padded_last, own_index, 0, keepdims=False)
    first_after = lax.dynamic_index_in_dim(padded_first, own_index + 2, 0, keepdims=False)
    return (last_before, first_after)


def coupled(boundary):
    devices = lax.axis_size("xs")
    gathered = lax.all_gather(boundary[None], "xs", axis=0, tiled=True)
    last_before, first_after = solve_gathered(gathered, lax.axis_index("xs"), devices)
    return (last_before, first_after)


def spike_parts(values, rate, own_index, devices):
    length = values.shape[0]
    position = lax.broadcasted_iota(jnp.int32, values.shape, 0)
    sub_band = jnp.where(position > 0, -rate, 0.0)
    super_band = jnp.where(position < length - 1, -rate, 0.0)
    centre = 1.0 + 2.0 * rate
    left_edge = jnp.where((position == 0) & (own_index > 0), -rate, 0.0)
    right_edge = jnp.where((position == length - 1) & (own_index < devices - 1), -rate, 0.0)
    stacked = jnp.stack([values, left_edge, right_edge], axis=1)
    solved = cyclic(sub_band[:, None], centre[:, None], super_band[:, None], stacked)
    particular = solved[:, 0]
    spike_left = solved[:, 1]
    spike_right = solved[:, 2]
    boundary = jnp.stack(
        [
            spike_left[0],
            spike_left[-1],
            spike_right[0],
            spike_right[-1],
            particular[0],
            particular[-1],
        ]
    )
    return (particular, spike_left, spike_right, boundary)


def eastward_solve(values, east_rate):
    particular, spike_left, spike_right, boundary = spike_parts(
        values, east_rate, lax.axis_index("xs"), lax.axis_size("xs")
    )
    last_before, first_after = coupled(boundary)
    return particular - spike_left * last_before[None] - spike_right * first_after[None]


def shards(source, eastward_rate, northward_rate, vertical_rate, amplitude):
    vertical_lines = jnp.moveaxis(vertical_rate, 1, 0)
    values = vertical_solve(source, vertical_lines)
    north_lines = lax.all_to_all(northward_rate, "pl", split_axis=1, concat_axis=2, tiled=True)
    values = to_planes(northward_solve(to_lines(values), north_lines))
    values = eastward_solve(values, eastward_rate)
    values = eastward_solve(values, eastward_rate)
    values = to_planes(northward_solve(to_lines(values), north_lines))
    values = vertical_solve(values, vertical_lines)
    return amplitude * values


def solution(mesh):
    placed = (
        P("xs", None, "pl"),
        P("xs", None, "pl"),
        P("xs", None, "pl"),
        P("xs", None, "pl"),
        P("xs", None, "pl"),
    )
    return jax.shard_map(
        shards, mesh=mesh, in_specs=placed, out_specs=P("xs", None, "pl"), check_vma=False
    )
```

profile of v0, /device:TPU:32, one launch (start us, length us, event | category | flops | bytes accessed | tf_op | source)
XLA Modules:
  0.0 218.9 jit_solution(4738351005885732317)
XLA Ops:
  3.7 7.0 %all-to-all-start = ((f32[32,16,128]{2,0,1:T(8,128)}), f32[32,16,128]{2,0,1:T(8,128)S(1)}, u32[]{:S(2)}, u32[]{:S(2)}) async-start(f32[32,16,128]{2,0,1:T(8,128)} %bitcast.68), calls=%async_computation | async-start | bytes 524288 | tf_op jit(solution)/shard_map/all_to_all | solution.py:86
  27.6 7.4 %all-to-all-start.1 = ((f32[32,16,128]{2,0,1:T(8,128)}), f32[32,16,128]{2,0,1:T(8,128)S(1)}, u32[]{:S(2)}, u32[]{:S(2)}) async-start(f32[32,16,128]{2,0,1:T(8,128)} %copy.1550), calls=%async_computation.1 | async-start | bytes 524288 | tf_op jit(solution)/shard_map/all_to_all | solution.py:257
  35.3 1.6 fusion.580
  37.8 5.9 %all-to-all-done.1 = f32[32,16,128]{2,0,1:T(8,128)S(1)} async-done(((f32[32,16,128]{2,0,1:T(8,128)}), f32[32,16,128]{2,0,1:T(8,128)S(1)}, u32[]{:S(2)}, u32[]{:S(2)}) %all-to-all-start.1) | async-done | bytes 262176 | tf_op jit(solution)/shard_map/all_to_all | solution.py:257
  44.1 1.6 fusion.579
  47.2 2.6 %copy_select_fusion = (f32[32,1,1024,2]{0,2,3,1:T(8,128)S(1)}, f32[32,1,1024,2]{0,2,3,1:T(8,128)S(1)}) fusion(f32[32,1,1024,2]{0,3,2,1:T(2,128)} %bitcast.4710, pred[1024,2]{0,1:T(4,128)(4,1)S(1)} %get-tuple-element.502, pred[1024,2]{0,1:T(4,128)(4,1)S(1)} %get-tuple-element.503), kind=kLoop, calls=%fused_computation.210 | loop fusion | flops 131072 | bytes 790528 | tf_op jit(solution)/shard_map/jit(_where)/select_n | solution.py:81
  61.8 1.9 copy.1628
  64.2 11.6 %reduce = f32[2048,32]{1,0:T(8,128)} reduce(f32[2048,1,32]{2,1,0:T(1,128)} %bitcast.4714, f32[]{:T(128)} %broadcast.2033), dimensions={1}, to_apply=%bitcast.4048.reduce_sub_computation | reduce | bytes 524292
  75.8 2.4 %reshape.3598 = f32[16,1,4096]{2,1,0:T(1,128)} reshape(f32[2048,32]{1,0:T(8,128)} %reduce) | data formatting | bytes 524288
  78.2 4.2 %all-to-all-start.2 = ((f32[16,1,4096]{2,1,0:T(1,128)}), f32[16,1,4096]{2,1,0:T(1,128)}, u32[]{:S(2)}, u32[]{:S(2)}) async-start(f32[16,1,4096]{2,1,0:T(1,128)} %reshape.3598), calls=%async_computation.2 | async-start | bytes 524288 | tf_op jit(solution)/shard_map/all_to_all | solution.py:90
  85.1 1.8 bitcast_divide_fusion.61
  86.9 4.2 %all-to-all-done.2 = f32[16,1,4096]{2,1,0:T(1,128)} async-done(((f32[16,1,4096]{2,1,0:T(1,128)}), f32[16,1,4096]{2,1,0:T(1,128)}, u32[]{:S(2)}, u32[]{:S(2)}) %all-to-all-start.2) | async-done | bytes 262176 | tf_op jit(solution)/shard_map/all_to_all | solution.py:90
  91.1 2.9 %reduce.1 = f32[16,4096]{1,0:T(8,128)} reduce(f32[16,1,4096]{2,1,0:T(1,128)} %all-to-all-done.2, f32[]{:T(128)} %broadcast.2033), dimensions={1}, to_apply=%all_to_all.14.reduce_sub_computation | reduce | bytes 524292 | tf_op jit(solution)/shard_map/all_to_all | solution.py:90
  93.9 3.7 %reshape.3599 = f32[2048,1,32]{2,1,0:T(1,128)} reshape(f32[16,4096]{1,0:T(8,128)} %reduce.1) | data formatting | bytes 524288
  97.7 3.4 %copy.1630 = f32[32,1,2048]{2,1,0:T(1,128)} copy(f32[32,1,2048]{0,1,2:T(1,128)} %bitcast.4711) | data formatting | bytes 524288 | tf_op jit(solution)/shard_map/all_to_all | solution.py:90
  104.9 20.5 %all-gather = f32[96,16,128]{2,1,0:T(8,128)S(1)} all-gather(f32[6,16,128]{2,1,0:T(8,128)S(1)} %constant_dynamic-update-slice_fusion), channel_id=2, replica_groups=mesh['pl'=16,'xs'=16] {'xs'}, dimensions={0}, use_global_device_ids=true | all-gather | bytes 835584 | tf_op jit(solution)/shard_map/all_gather | solution.py:215
  130.9 5.1 %fusion.406 = (f32[16,16,128]{2,1,0:T(8,128)S(1)}, f32[16,16,128]{2,1,0:T(8,128)S(1)}, f32[16,16,128]{2,1,0:T(8,128)S(1)}, f32[16,16,128]{2,1,0:T(8,128)S(1)}, f...) fusion(f32[16,16,128]{2,1,0:T(8,128)S(1)} %get-tuple-element.322, ...), kind=kLoop, calls=%fused_computation.1275 | loop fusion | flops 23101440 | bytes 16613376 | tf_op jit(solution)/shard_map/add | solution.py:115
  138.8 18.6 %all-gather.1 = f32[96,16,128]{2,1,0:T(8,128)S(1)} all-gather(f32[6,16,128]{2,1,0:T(8,128)S(1)} %constant_dynamic-update-slice_fusion.56), channel_id=3, replica_groups=mesh['pl'=16,'xs'=16] {'xs'}, dimensions={0}, use_global_device_ids=true | all-gather | bytes 835584 | tf_op jit(solution)/shard_map/all_gather | solution.py:215
  162.9 5.0 %fusion.403 = (f32[16,16,128]{2,1,0:T(8,128)S(1)}, f32[16,16,128]{2,1,0:T(8,128)S(1)}, f32[16,16,128]{2,1,0:T(8,128)S(1)}, f32[16,16,128]{2,1,0:T(8,128)S(1)}, f...) fusion(f32[16,16,128]{2,1,0:T(8,128)S(1)} %get-tuple-element.316, ...), kind=kLoop, calls=%fused_computation.1183 | loop fusion | flops 23101440 | bytes 16613376 | tf_op jit(solution)/shard_map/add | solution.py:115
  168.2 12.3 %all_to_all.23 = f32[32,16,128]{2,0,1:T(8,128)S(1)} all-to-all(f32[32,16,128]{2,0,1:T(8,128)S(1)} %copy.1714), channel_id=1, replica_groups=mesh['pl'=16,'xs'=16] {'pl'}, dimensions={1} | all-to-all | bytes 524288 | tf_op jit(solution)/shard_map/all_to_all | solution.py:86
  181.8 2.5 %fusion.578 = (f32[32,1,1024,1]{0,3,2,1:T(1,128)S(1)}, f32[32,1,1024,1]{0,3,2,1:T(1,128)S(1)}) fusion(f32[32,1,1024,2]{0,3,2,1:T(2,128)} %bitcast.4715), kind=kLoop, calls=%fused_computation.1763 | loop fusion | bytes 524288 | tf_op jit(solution)/shard_map/slice | solution.py:43
  190.6 9.3 %reduce.2 = f32[2048,32]{1,0:T(8,128)S(1)} reduce(f32[2048,1,32]{2,1,0:T(1,128)S(1)} %bitcast.4716, f32[]{:T(128)} %broadcast.2033), dimensions={1}, to_apply=%bitcast.4050.reduce_sub_computation | reduce | bytes 524292
  200.4 11.8 %all_to_all.24 = f32[16,1,4096]{2,1,0:T(1,128)S(1)} all-to-all(f32[16,1,4096]{2,1,0:T(1,128)S(1)} %reshape.3600), channel_id=1, replica_groups=mesh['pl'=16,'xs'=16] {'pl'}, dimensions={0} | all-to-all | bytes 524288 | tf_op jit(solution)/shard_map/all_to_all | solution.py:90
  213.4 1.8 reshape.3601
  (894 shorter events, 63.7 us)
Async XLA Ops:
  2.3 8.4 %copy-start.113 = (f32[32,16,128]{2,1,0:T(8,128)S(1)}, f32[32,16,128]{2,1,0:T(8,128)}, u32[]{:S(2)}) copy-start(f32[32,16,128]{2,1,0:T(8,128)} %param.6) | copy-start | bytes 786436
  3.7 23.9 %all-to-all-start = ((f32[32,16,128]{2,0,1:T(8,128)}), f32[32,16,128]{2,0,1:T(8,128)S(1)}, u32[]{:S(2)}, u32[]{:S(2)}) async-start(f32[32,16,128]{2,0,1:T(8,128)} %bitcast.68), calls=%async_computation | async-start | bytes 524288 | tf_op jit(solution)/shard_map/all_to_all | solution.py:86
  13.6 12.6 %copy-start.112 = (f32[32,16,128]{2,1,0:T(8,128)S(1)}, f32[32,16,128]{2,1,0:T(8,128)}, u32[]{:S(2)}) copy-start(f32[32,16,128]{2,1,0:T(8,128)} %param.7) | copy-start | bytes 786436
  27.6 16.1 %all-to-all-start.1 = ((f32[32,16,128]{2,0,1:T(8,128)}), f32[32,16,128]{2,0,1:T(8,128)S(1)}, u32[]{:S(2)}, u32[]{:S(2)}) async-start(f32[32,16,128]{2,0,1:T(8,128)} %copy.1550), calls=%async_computation.1 | async-start | bytes 524288 | tf_op jit(solution)/shard_map/all_to_all | solution.py:257
  52.8 8.1 %copy-start.2 = (f32[32,1,512,1]{0,3,2,1:T(1,128)}, f32[32,1,512,1]{0,3,2,1:T(1,128)S(1)}, u32[]{:S(2)}) copy-start(f32[32,1,512,1]{0,3,2,1:T(1,128)S(1)} %get-tuple-element.347) | copy-start | bytes 196612
  53.3 7.6 %copy-start.4 = (f32[32,1,512,1]{0,3,2,1:T(1,128)}, f32[32,1,512,1]{0,3,2,1:T(1,128)S(1)}, u32[]{:S(2)}) copy-start(f32[32,1,512,1]{0,3,2,1:T(1,128)S(1)} %get-tuple-element.343) | copy-start | bytes 196612
  54.6 5.9 %copy-start.16 = (f32[32,1,256,1]{0,3,2,1:T(1,128)}, f32[32,1,256,1]{0,3,2,1:T(1,128)S(1)}, u32[]{:S(2)}) copy-start(f32[32,1,256,1]{0,3,2,1:T(1,128)S(1)} %get-tuple-element.372) | copy-start | bytes 98308
  54.8 5.7 %copy-start.18 = (f32[32,1,256,1]{0,3,2,1:T(1,128)}, f32[32,1,256,1]{0,3,2,1:T(1,128)S(1)}, u32[]{:S(2)}) copy-start(f32[32,1,256,1]{0,3,2,1:T(1,128)S(1)} %get-tuple-element.368) | copy-start | bytes 98308
  55.3 5.0 %copy-start.14 = (f32[32,1,128,1]{0,3,2,1:T(1,128)}, f32[32,1,128,1]{0,3,2,1:T(1,128)S(1)}, u32[]{:S(2)}) copy-start(f32[32,1,128,1]{0,3,2,1:T(1,128)S(1)} %get-tuple-element.399) | copy-start | bytes 49156
  55.7 4.6 %copy-start.41 = (f32[32,1,128,1]{0,3,2,1:T(1,128)}, f32[32,1,128,1]{0,3,2,1:T(1,128)S(1)}, u32[]{:S(2)}) copy-start(f32[32,1,128,1]{0,3,2,1:T(1,128)S(1)} %get-tuple-element.400) | copy-start | bytes 49156
  55.8 4.5 %copy-start.43 = (f32[32,1,128,1]{0,3,2,1:T(1,128)}, f32[32,1,128,1]{0,3,2,1:T(1,128)S(1)}, u32[]{:S(2)}) copy-start(f32[32,1,128,1]{0,3,2,1:T(1,128)S(1)} %get-tuple-element.396) | copy-start | bytes 49156
  56.1 4.0 %copy-start.35 = (f32[32,1,64,1]{0,3,2,1:T(1,128)}, f32[32,1,64,1]{0,3,2,1:T(1,128)S(1)}, u32[]{:S(2)}) copy-start(f32[32,1,64,1]{0,3,2,1:T(1,128)S(1)} %get-tuple-element.417) | copy-start | bytes 24580
  56.6 3.6 %copy-start.67 = (f32[32,1,64,1]{0,3,2,1:T(1,128)}, f32[32,1,64,1]{0,3,2,1:T(1,128)S(1)}, u32[]{:S(2)}) copy-start(f32[32,1,64,1]{0,3,2,1:T(1,128)S(1)} %get-tuple-element.418) | copy-start | bytes 24580
  56.6 3.6 %copy-start.71 = (f32[32,1,64,1]{0,3,2,1:T(1,128)}, f32[32,1,64,1]{0,3,2,1:T(1,128)S(1)}, u32[]{:S(2)}) copy-start(f32[32,1,64,1]{0,3,2,1:T(1,128)S(1)} %get-tuple-element.419) | copy-start | bytes 24580
  56.7 3.7 %copy-start.69 = (f32[32,1,64,1]{0,3,2,1:T(1,128)}, f32[32,1,64,1]{0,3,2,1:T(1,128)S(1)}, u32[]{:S(2)}) copy-start(f32[32,1,64,1]{0,3,2,1:T(1,128)S(1)} %get-tuple-element.414) | copy-start | bytes 24580
  56.7 3.7 %copy-start.100 = (f32[32,1,64]{0,2,1:T(8,128)}, f32[32,1,64]{0,2,1:T(8,128)S(1)}, u32[]{:S(2)}) copy-start(f32[32,1,64]{0,2,1:T(8,128)S(1)} %get-tuple-element.236) | copy-start | bytes 24580
  56.9 3.2 %copy-start.88 = (f32[32,1,32,1]{0,3,2,1:T(1,128)}, f32[32,1,32,1]{0,3,2,1:T(1,128)S(1)}, u32[]{:S(2)}) copy-start(f32[32,1,32,1]{0,3,2,1:T(1,128)S(1)} %get-tuple-element.434) | copy-start | bytes 12292
  64.2 18.8 %copy-start.60 = (f32[16,1,1,16,128]{4,1,0,3,2:T(1,128)S(1)}, f32[16,1,1,16,128]{4,1,0,3,2:T(1,128)}, u32[]{:S(2)}) copy-start(f32[16,1,1,16,128]{4,1,0,3,2:T(1,128)} %copy-done.59) | copy-start | bytes 393220
  64.2 19.5 %copy-start.64 = (f32[32,16,128]{2,0,1:T(8,128)S(1)}, f32[32,16,128]{2,0,1:T(8,128)}, u32[]{:S(2)}) copy-start(f32[32,16,128]{2,0,1:T(8,128)} %get-tuple-element.364) | copy-start | bytes 786436
  78.2 12.9 %all-to-all-start.2 = ((f32[16,1,4096]{2,1,0:T(1,128)}), f32[16,1,4096]{2,1,0:T(1,128)}, u32[]{:S(2)}, u32[]{:S(2)}) async-start(f32[16,1,4096]{2,1,0:T(1,128)} %reshape.3598), calls=%async_computation.2 | async-start | bytes 524288 | tf_op jit(solution)/shard_map/all_to_all | solution.py:90
  83.9 17.2 %copy-start.30 = (f32[32,16,128]{2,1,0:T(8,128)}, f32[32,16,128]{2,1,0:T(8,128)S(1)}, u32[]{:S(2)}) copy-start(f32[32,16,128]{2,1,0:T(8,128)S(1)} %copy.1633) | copy-start | bytes 786436
  85.1 17.0 %copy-start.32 = (f32[32,16,128]{2,1,0:T(8,128)}, f32[32,16,128]{2,1,0:T(8,128)S(1)}, u32[]{:S(2)}) copy-start(f32[32,16,128]{2,1,0:T(8,128)S(1)} %copy.1632) | copy-start | bytes 786436
  104.7 20.8 %copy-start = (f32[14,16,16,128]{3,2,1,0:T(8,128)S(1)}, f32[14,16,16,128]{3,2,1,0:T(8,128)}, u32[]{:S(2)}) copy-start(f32[14,16,16,128]{3,2,1,0:T(8,128)} %constant_dynamic-update-slice_fusion.13) | copy-start | bytes 5505028
  138.7 18.9 %copy-start.1 = (f32[14,16,16,128]{3,2,1,0:T(8,128)S(1)}, f32[14,16,16,128]{3,2,1,0:T(8,128)}, u32[]{:S(2)}) copy-start(f32[14,16,16,128]{3,2,1,0:T(8,128)} %constant_dynamic-update-slice_fusion.69) | copy-start | bytes 5505028
  (161 other events, 198.9 us)
where the time goes:
time: 223 us; the launch traced here: 219 us
  other arithmetic  63.6 us (29%)
  blocking collectives  63.3 us (28%)
  local copies, waits for them, and re-layouts  57.4 us (26%)
  starting transfers between devices  18.6 us (8%)
  waiting for transfers between devices  10 us (4%)
  between operations  6 us (3%)
    all_gather x2, blocking collectives, coupled(): gathered = lax.all_gather(boundary[None], 'xs', axis=0, tiled=True)  39.2 us
    unnamed x80, other arithmetic  26.3 us
    unnamed x406, local copies, waits for them, and re-layouts  21.7 us
    all_to_all x1, blocking collectives, to_lines(): return lax.all_to_all(values, 'pl', split_axis=1, concat_axis=2, tiled=True)  12.3 us
    all_to_all x1, blocking collectives, to_planes(): return lax.all_to_all(values, 'pl', split_axis=2, concat_axis=1, tiled=True)  11.8 us
    add x2, other arithmetic, matrix_vector(): matrix[2] * vector[0] + matrix[3] * vector[1]  10.1 us
    slice x42, local copies, waits for them, and re-layouts, halves(): return (paired[..., 0], paired[..., 1])  9.86 us
    all_to_all x1, starting transfers between devices, shards(): lax.all_to_all(northward_rate, 'pl', split_axis=1, concat_axis=2, tiled=T...  7.38 us
  transfers between devices with their start and end apart: 3, of which 2 were waited for; matrix products, arithmetic and copies ran while one was open for 11% of the time, Pallas kernels for 0%

commit v1 on v0

--- a/solution.py
+++ b/solution.py
@@ -83,7 +83,10 @@
 
 
 def to_lines(values):
-    return lax.all_to_all(values, "pl", split_axis=1, concat_axis=2, tiled=True)
+    return jnp.concatenate(
+        lax.all_to_all(jnp.stack(jnp.split(values, lax.axis_size("pl"), axis=1)), "pl", 0, 0),
+        axis=2,
+    )
 
 
 def to_planes(values):

time: 223 us -> 232 us (1.040)
  local copies, waits for them, and re-layouts: 57.4 us -> 66 us
    unnamed x406 -> x428, local copies, waits for them, and re-layouts: 21.7 us -> 30.4 us
where the time goes in v1:
time: 232 us; the launch traced here: 228 us
  local copies, waits for them, and re-layouts  66 us (28%)
  other arithmetic  63.7 us (27%)
  blocking collectives  63.3 us (27%)
  starting transfers between devices  18.6 us (8%)
  waiting for transfers between devices  10.2 us (4%)
  between operations  6.2 us (3%)
    all_gather x2, blocking collectives, coupled(): gathered = lax.all_gather(boundary[None], 'xs', axis=0, tiled=True)  39.2 us
    unnamed x428, local copies, waits for them, and re-layouts  30.4 us
    unnamed x80, other arithmetic  26.3 us
    all_to_all x1, blocking collectives, to_lines(): lax.all_to_all(jnp.stack(jnp.split(values, lax.axis_size('pl'), axis=1)),...  12.3 us
    all_to_all x1, blocking collectives, to_planes(): return lax.all_to_all(values, 'pl', split_axis=2, concat_axis=1, tiled=True)  11.8 us
    add x2, other arithmetic, matrix_vector(): matrix[2] * vector[0] + matrix[3] * vector[1]  10.1 us
    slice x42, local copies, waits for them, and re-layouts, halves(): return (paired[..., 0], paired[..., 1])  9.9 us
    all_to_all x1, starting transfers between devices, shards(): lax.all_to_all(northward_rate, 'pl', split_axis=1, concat_axis=2, tiled=T...  7.38 us
  transfers between devices with their start and end apart: 3, of which 2 were waited for; matrix products, arithmetic and copies ran while one was open for 11% of the time, Pallas kernels for 0%

profile of v1, /device:TPU:32, one launch (start us, length us, event | category | flops | bytes accessed | tf_op | source)
XLA Modules:
  0.0 228.0 jit_solution(1565510878924117892)
XLA Ops:
  13.0 7.0 %all-to-all-start = ((f32[16,32,1,128]{3,1,2,0:T(8,128)}), f32[16,32,1,128]{3,1,2,0:T(8,128)S(1)}, u32[]{:S(2)}, u32[]{:S(2)}) async-start(f32[16,32,1,128]{3,1,2,0:T(8,128)} %constant_dynamic-update-slice_fusion), calls=%async_computation | async-start | bytes 524288 | tf_op jit(solution)/shard_map/all_to_all | solution.py:87
  37.1 7.4 %all-to-all-start.1 = ((f32[32,16,128]{2,0,1:T(8,128)}), f32[32,16,128]{2,0,1:T(8,128)S(1)}, u32[]{:S(2)}, u32[]{:S(2)}) async-start(f32[32,16,128]{2,0,1:T(8,128)} %copy.1638), calls=%async_computation.1 | async-start | bytes 524288 | tf_op jit(solution)/shard_map/all_to_all | solution.py:260
  44.9 1.6 fusion.580
  47.3 5.9 %all-to-all-done.1 = f32[32,16,128]{2,0,1:T(8,128)S(1)} async-done(((f32[32,16,128]{2,0,1:T(8,128)}), f32[32,16,128]{2,0,1:T(8,128)S(1)}, u32[]{:S(2)}, u32[]{:S(2)}) %all-to-all-start.1) | async-done | bytes 262176 | tf_op jit(solution)/shard_map/all_to_all | solution.py:260
  53.6 1.6 fusion.579
  56.7 2.6 %copy_select_fusion = (f32[32,1,1024,2]{0,2,3,1:T(8,128)S(1)}, f32[32,1,1024,2]{0,2,3,1:T(8,128)S(1)}) fusion(f32[32,1,1024,2]{0,3,2,1:T(2,128)} %bitcast.4822, pred[1024,2]{0,1:T(4,128)(4,1)S(1)} %get-tuple-element.518, pred[1024,2]{0,1:T(4,128)(4,1)S(1)} %get-tuple-element.519), kind=kLoop, calls=%fused_computation.210 | loop fusion | flops 131072 | bytes 790528 | tf_op jit(solution)/shard_map/jit(_where)/select_n | solution.py:81
  71.3 1.9 copy.1716
  73.7 11.6 %reduce = f32[2048,32]{1,0:T(8,128)} reduce(f32[2048,1,32]{2,1,0:T(1,128)} %bitcast.4826, f32[]{:T(128)} %broadcast.2033), dimensions={1}, to_apply=%bitcast.4160.reduce_sub_computation | reduce | bytes 524292
  85.3 2.4 %reshape.3590 = f32[16,1,4096]{2,1,0:T(1,128)} reshape(f32[2048,32]{1,0:T(8,128)} %reduce) | data formatting | bytes 524288
  87.7 4.2 %all-to-all-start.2 = ((f32[16,1,4096]{2,1,0:T(1,128)}), f32[16,1,4096]{2,1,0:T(1,128)}, u32[]{:S(2)}, u32[]{:S(2)}) async-start(f32[16,1,4096]{2,1,0:T(1,128)} %reshape.3590), calls=%async_computation.2 | async-start | bytes 524288 | tf_op jit(solution)/shard_map/all_to_all | solution.py:93
  94.6 1.7 bitcast_divide_fusion.61
  96.3 4.3 %all-to-all-done.2 = f32[16,1,4096]{2,1,0:T(1,128)} async-done(((f32[16,1,4096]{2,1,0:T(1,128)}), f32[16,1,4096]{2,1,0:T(1,128)}, u32[]{:S(2)}, u32[]{:S(2)}) %all-to-all-start.2) | async-done | bytes 262176 | tf_op jit(solution)/shard_map/all_to_all | solution.py:93
  100.6 2.9 %reduce.1 = f32[16,4096]{1,0:T(8,128)} reduce(f32[16,1,4096]{2,1,0:T(1,128)} %all-to-all-done.2, f32[]{:T(128)} %broadcast.2033), dimensions={1}, to_apply=%all_to_all.14.reduce_sub_computation | reduce | bytes 524292 | tf_op jit(solution)/shard_map/all_to_all | solution.py:93
  103.5 3.8 %reshape.3591 = f32[2048,1,32]{2,1,0:T(1,128)} reshape(f32[16,4096]{1,0:T(8,128)} %reduce.1) | data formatting | bytes 524288
  107.3 3.4 %copy.1718 = f32[32,1,2048]{2,1,0:T(1,128)} copy(f32[32,1,2048]{0,1,2:T(1,128)} %bitcast.4823) | data formatting | bytes 524288 | tf_op jit(solution)/shard_map/all_to_all | solution.py:93
  114.5 20.5 %all-gather = f32[96,16,128]{2,1,0:T(8,128)S(1)} all-gather(f32[6,16,128]{2,1,0:T(8,128)S(1)} %constant_dynamic-update-slice_fusion.16), channel_id=2, replica_groups=mesh['pl'=16,'xs'=16] {'xs'}, dimensions={0}, use_global_device_ids=true | all-gather | bytes 835584 | tf_op jit(solution)/shard_map/all_gather | solution.py:218
  140.4 5.1 %fusion.406 = (f32[16,16,128]{2,1,0:T(8,128)S(1)}, f32[16,16,128]{2,1,0:T(8,128)S(1)}, f32[16,16,128]{2,1,0:T(8,128)S(1)}, f32[16,16,128]{2,1,0:T(8,128)S(1)}, f...) fusion(f32[16,16,128]{2,1,0:T(8,128)S(1)} %get-tuple-element.322, ...), kind=kLoop, calls=%fused_computation.1307 | loop fusion | flops 23101440 | bytes 16613376 | tf_op jit(solution)/shard_map/add | solution.py:118
  147.5 18.6 %all-gather.1 = f32[96,16,128]{2,1,0:T(8,128)S(1)} all-gather(f32[6,16,128]{2,1,0:T(8,128)S(1)} %constant_dynamic-update-slice_fusion.74), channel_id=3, replica_groups=mesh['pl'=16,'xs'=16] {'xs'}, dimensions={0}, use_global_device_ids=true | all-gather | bytes 835584 | tf_op jit(solution)/shard_map/all_gather | solution.py:218
  171.6 5.0 %fusion.403 = (f32[16,16,128]{2,1,0:T(8,128)S(1)}, f32[16,16,128]{2,1,0:T(8,128)S(1)}, f32[16,16,128]{2,1,0:T(8,128)S(1)}, f32[16,16,128]{2,1,0:T(8,128)S(1)}, f...) fusion(f32[16,16,128]{2,1,0:T(8,128)S(1)} %get-tuple-element.316, ...), kind=kLoop, calls=%fused_computation.1215 | loop fusion | flops 23101440 | bytes 16613376 | tf_op jit(solution)/shard_map/add | solution.py:118
  177.2 12.3 %all_to_all.40 = f32[16,32,1,128]{3,1,2,0:T(8,128)S(1)} all-to-all(f32[16,32,1,128]{3,1,2,0:T(8,128)S(1)} %constant_dynamic-update-slice_fusion.132), channel_id=1, replica_groups=mesh['pl'=16,'xs'=16] {'pl'}, dimensions={0} | all-to-all | bytes 524288 | tf_op jit(solution)/shard_map/all_to_all | solution.py:87
  190.8 2.6 %fusion.578 = (f32[32,1,1024,1]{0,3,2,1:T(1,128)S(1)}, f32[32,1,1024,1]{0,3,2,1:T(1,128)S(1)}) fusion(f32[32,1,1024,2]{0,3,2,1:T(2,128)} %bitcast.4827), kind=kLoop, calls=%fused_computation.1811 | loop fusion | bytes 524288 | tf_op jit(solution)/shard_map/slice | solution.py:43
  199.7 9.3 %reduce.2 = f32[2048,32]{1,0:T(8,128)S(1)} reduce(f32[2048,1,32]{2,1,0:T(1,128)S(1)} %bitcast.4828, f32[]{:T(128)} %broadcast.2033), dimensions={1}, to_apply=%bitcast.4162.reduce_sub_computation | reduce | bytes 524292
  209.5 11.8 %all_to_all.41 = f32[16,1,4096]{2,1,0:T(1,128)S(1)} all-to-all(f32[16,1,4096]{2,1,0:T(1,128)S(1)} %reshape.3592), channel_id=1, replica_groups=mesh['pl'=16,'xs'=16] {'pl'}, dimensions={0} | all-to-all | bytes 524288 | tf_op jit(solution)/shard_map/all_to_all | solution.py:93
  222.5 1.8 reshape.3593
  (918 shorter events, 72.4 us)
Async XLA Ops:
  3.0 17.1 %copy-start.109 = (f32[32,16,128]{2,1,0:T(8,128)S(1)}, f32[32,16,128]{2,1,0:T(8,128)}, u32[]{:S(2)}) copy-start(f32[32,16,128]{2,1,0:T(8,128)} %param.6) | copy-start | bytes 786436
  13.0 24.2 %all-to-all-start = ((f32[16,32,1,128]{3,1,2,0:T(8,128)}), f32[16,32,1,128]{3,1,2,0:T(8,128)S(1)}, u32[]{:S(2)}, u32[]{:S(2)}) async-start(f32[16,32,1,128]{3,1,2,0:T(8,128)} %constant_dynamic-update-slice_fusion), calls=%async_computation | async-start | bytes 524288 | tf_op jit(solution)/shard_map/all_to_all | solution.py:87
  22.9 12.8 %copy-start.108 = (f32[32,16,128]{2,1,0:T(8,128)S(1)}, f32[32,16,128]{2,1,0:T(8,128)}, u32[]{:S(2)}) copy-start(f32[32,16,128]{2,1,0:T(8,128)} %param.7) | copy-start | bytes 786436
  37.1 16.1 %all-to-all-start.1 = ((f32[32,16,128]{2,0,1:T(8,128)}), f32[32,16,128]{2,0,1:T(8,128)S(1)}, u32[]{:S(2)}, u32[]{:S(2)}) async-start(f32[32,16,128]{2,0,1:T(8,128)} %copy.1638), calls=%async_computation.1 | async-start | bytes 524288 | tf_op jit(solution)/shard_map/all_to_all | solution.py:260
  62.3 8.1 %copy-start.2 = (f32[32,1,512,1]{0,3,2,1:T(1,128)}, f32[32,1,512,1]{0,3,2,1:T(1,128)S(1)}, u32[]{:S(2)}) copy-start(f32[32,1,512,1]{0,3,2,1:T(1,128)S(1)} %get-tuple-element.347) | copy-start | bytes 196612
  62.8 7.6 %copy-start.4 = (f32[32,1,512,1]{0,3,2,1:T(1,128)}, f32[32,1,512,1]{0,3,2,1:T(1,128)S(1)}, u32[]{:S(2)}) copy-start(f32[32,1,512,1]{0,3,2,1:T(1,128)S(1)} %get-tuple-element.343) | copy-start | bytes 196612
  64.1 5.9 %copy-start.16 = (f32[32,1,256,1]{0,3,2,1:T(1,128)}, f32[32,1,256,1]{0,3,2,1:T(1,128)S(1)}, u32[]{:S(2)}) copy-start(f32[32,1,256,1]{0,3,2,1:T(1,128)S(1)} %get-tuple-element.388) | copy-start | bytes 98308
  64.4 5.7 %copy-start.18 = (f32[32,1,256,1]{0,3,2,1:T(1,128)}, f32[32,1,256,1]{0,3,2,1:T(1,128)S(1)}, u32[]{:S(2)}) copy-start(f32[32,1,256,1]{0,3,2,1:T(1,128)S(1)} %get-tuple-element.384) | copy-start | bytes 98308
  64.8 5.0 %copy-start.14 = (f32[32,1,128,1]{0,3,2,1:T(1,128)}, f32[32,1,128,1]{0,3,2,1:T(1,128)S(1)}, u32[]{:S(2)}) copy-start(f32[32,1,128,1]{0,3,2,1:T(1,128)S(1)} %get-tuple-element.415) | copy-start | bytes 49156
  65.2 4.6 %copy-start.37 = (f32[32,1,128,1]{0,3,2,1:T(1,128)}, f32[32,1,128,1]{0,3,2,1:T(1,128)S(1)}, u32[]{:S(2)}) copy-start(f32[32,1,128,1]{0,3,2,1:T(1,128)S(1)} %get-tuple-element.416) | copy-start | bytes 49156
  65.3 4.5 %copy-start.39 = (f32[32,1,128,1]{0,3,2,1:T(1,128)}, f32[32,1,128,1]{0,3,2,1:T(1,128)S(1)}, u32[]{:S(2)}) copy-start(f32[32,1,128,1]{0,3,2,1:T(1,128)S(1)} %get-tuple-element.412) | copy-start | bytes 49156
  65.6 4.0 %copy-start.31 = (f32[32,1,64,1]{0,3,2,1:T(1,128)}, f32[32,1,64,1]{0,3,2,1:T(1,128)S(1)}, u32[]{:S(2)}) copy-start(f32[32,1,64,1]{0,3,2,1:T(1,128)S(1)} %get-tuple-element.433) | copy-start | bytes 24580
  66.1 3.6 %copy-start.63 = (f32[32,1,64,1]{0,3,2,1:T(1,128)}, f32[32,1,64,1]{0,3,2,1:T(1,128)S(1)}, u32[]{:S(2)}) copy-start(f32[32,1,64,1]{0,3,2,1:T(1,128)S(1)} %get-tuple-element.434) | copy-start | bytes 24580
  66.1 3.6 %copy-start.67 = (f32[32,1,64,1]{0,3,2,1:T(1,128)}, f32[32,1,64,1]{0,3,2,1:T(1,128)S(1)}, u32[]{:S(2)}) copy-start(f32[32,1,64,1]{0,3,2,1:T(1,128)S(1)} %get-tuple-element.435) | copy-start | bytes 24580
  66.2 3.7 %copy-start.65 = (f32[32,1,64,1]{0,3,2,1:T(1,128)}, f32[32,1,64,1]{0,3,2,1:T(1,128)S(1)}, u32[]{:S(2)}) copy-start(f32[32,1,64,1]{0,3,2,1:T(1,128)S(1)} %get-tuple-element.430) | copy-start | bytes 24580
  66.2 3.7 %copy-start.96 = (f32[32,1,64]{0,2,1:T(8,128)}, f32[32,1,64]{0,2,1:T(8,128)S(1)}, u32[]{:S(2)}) copy-start(f32[32,1,64]{0,2,1:T(8,128)S(1)} %get-tuple-element.236) | copy-start | bytes 24580
  66.4 3.1 %copy-start.80 = (f32[32,1,32,1]{0,3,2,1:T(1,128)}, f32[32,1,32,1]{0,3,2,1:T(1,128)S(1)}, u32[]{:S(2)}) copy-start(f32[32,1,32,1]{0,3,2,1:T(1,128)S(1)} %get-tuple-element.449) | copy-start | bytes 12292
  66.4 3.2 %copy-start.84 = (f32[32,1,32,1]{0,3,2,1:T(1,128)}, f32[32,1,32,1]{0,3,2,1:T(1,128)S(1)}, u32[]{:S(2)}) copy-start(f32[32,1,32,1]{0,3,2,1:T(1,128)S(1)} %get-tuple-element.450) | copy-start | bytes 12292
  66.5 3.0 %copy-start.82 = (f32[32,1,32,1]{0,3,2,1:T(1,128)}, f32[32,1,32,1]{0,3,2,1:T(1,128)S(1)}, u32[]{:S(2)}) copy-start(f32[32,1,32,1]{0,3,2,1:T(1,128)S(1)} %get-tuple-element.445) | copy-start | bytes 12292
  73.7 18.9 %copy-start.56 = (f32[16,1,1,16,128]{4,1,0,3,2:T(1,128)S(1)}, f32[16,1,1,16,128]{4,1,0,3,2:T(1,128)}, u32[]{:S(2)}) copy-start(f32[16,1,1,16,128]{4,1,0,3,2:T(1,128)} %copy-done.55) | copy-start | bytes 393220
  73.7 19.6 %copy-start.60 = (f32[32,16,128]{2,0,1:T(8,128)S(1)}, f32[32,16,128]{2,0,1:T(8,128)}, u32[]{:S(2)}) copy-start(f32[32,16,128]{2,0,1:T(8,128)} %get-tuple-element.380) | copy-start | bytes 786436
  87.7 12.9 %all-to-all-start.2 = ((f32[16,1,4096]{2,1,0:T(1,128)}), f32[16,1,4096]{2,1,0:T(1,128)}, u32[]{:S(2)}, u32[]{:S(2)}) async-start(f32[16,1,4096]{2,1,0:T(1,128)} %reshape.3590), calls=%async_computation.2 | async-start | bytes 524288 | tf_op jit(solution)/shard_map/all_to_all | solution.py:93
  114.3 20.8 %copy-start = (f32[14,16,16,128]{3,2,1,0:T(8,128)S(1)}, f32[14,16,16,128]{3,2,1,0:T(8,128)}, u32[]{:S(2)}) copy-start(f32[14,16,16,128]{3,2,1,0:T(8,128)} %constant_dynamic-update-slice_fusion.31) | copy-start | bytes 5505028
  147.4 18.9 %copy-start.1 = (f32[14,16,16,128]{3,2,1,0:T(8,128)S(1)}, f32[14,16,16,128]{3,2,1,0:T(8,128)}, u32[]{:S(2)}) copy-start(f32[14,16,16,128]{3,2,1,0:T(8,128)} %constant_dynamic-update-slice_fusion.89) | copy-start | bytes 5505028
  (157 other events, 196.2 us)
